TPU v7x, 32 devices: a whole 2x2x4 slice. The times are simulated.
32 devices in a mesh: node: 8 (over z, x), feat: 4 (over y, core).
Axes of the slice: x: 2, y: 2, z: 4, core: 2. Of those that a mesh axis runs over, the one named last changes fastest.
Arguments:
- features: bfloat16 [256, 4096], P('feat', 'node'), may hold values from -6 to 6
- tile_values: bfloat16 [256, 128, 128], P('node'), may hold values from -0.1875 to 0.1875
- tile_rows: int32 [64, 4], P('node'), may hold values from 0 to 3
- tile_cols: int32 [64, 4], P('node'), may hold values from 0 to 3
- tile_counts: int32 [64], P('node'), may hold values from 0 to 4, as said below
- weight: bfloat16 [256, 256], replicated, may hold values from -0.375 to 0.375
- cotangent: bfloat16 [256, 4096], P(None, ('node', 'feat')), may hold values from -6 to 6
Outputs:
- activated: bfloat16 [256, 4096], P(None, ('node', 'feat'))
- grad_weight: float32 [256, 256], replicated
- grad_features: float32 [256, 4096], P('feat', 'node')
Inputs may be any that keep to these rules, and one draw needn't show every extreme that they name: `tile_counts`: slots at or past a pair's count are ignored; some pair has all 4 slots live, and the live slots of one receiving node index vary strongly between indices.
All inputs are finite; a program needn't handle non-finite values.
Results may differ from a plain program's by a relative error of at most 0.012.
Values may be sent and summed in bfloat16 or wider, within the bound.
No kernel may reach another device: no remote copies, remote signals or barrier semaphores. Data moves between devices by JAX's collectives and lax.ppermute only.
A program may use at most 64 MiB of HBM per device.

v0:
```python
import jax
import jax.numpy as jnp
from jax import lax
from jax.sharding import PartitionSpec as P


def passed_along(x, axis, by):
    count = lax.axis_size(axis)
    return lax.ppermute(x, axis, [(i, (i + by) % count) for i in range(count)])


def select_pair(tile_values, tile_rows, tile_cols, tile_counts, source):
    slots = tile_rows.shape[1]
    values = lax.dynamic_slice_in_dim(tile_values, source * slots, slots, 0)
    row_ids = lax.dynamic_index_in_dim(tile_rows, source, 0, keepdims=False)
    col_ids = lax.dynamic_index_in_dim(tile_cols, source, 0, keepdims=False)
    number = lax.dynamic_index_in_dim(tile_counts, source, 0, keepdims=False)
    live = (jnp.arange(slots) < number).astype(jnp.float32)
    return (values, row_ids, col_ids, live)


def add_forward(totals, piece, parts, keep):
    values, row_ids, col_ids, live = parts
    blocks_in = piece.reshape(piece.shape[0], -1, values.shape[1])
    block_count = blocks_in.shape[1]
    pick = jax.nn.one_hot(col_ids, block_count, dtype=jnp.bfloat16)
    chosen = jnp.einsum("frm,sr->fsm", blocks_in, pick, preferred_element_type=jnp.float32).astype(
        jnp.bfloat16
    )
    product = jnp.einsum("fsm,sjm->fsj", chosen, values, preferred_element_type=jnp.float32)
    place = jax.nn.one_hot(row_ids, block_count, dtype=jnp.float32) * (live * keep)[:, None]
    return totals + jnp.einsum("fsj,sr->frj", product, place)


def add_backward(totals, grad_blocks, parts, keep):
    values, row_ids, col_ids, live = parts
    block_count = grad_blocks.shape[1]
    pick = jax.nn.one_hot(row_ids, block_count, dtype=jnp.bfloat16)
    chosen = jnp.einsum(
        "frj,sr->fsj", grad_blocks, pick, preferred_element_type=jnp.float32
    ).astype(jnp.bfloat16)
    product = jnp.einsum("fsj,sjm->fsm", chosen, values, preferred_element_type=jnp.float32)
    place = jax.nn.one_hot(col_ids, block_count, dtype=jnp.float32) * (live * keep)[:, None]
    return totals + jnp.einsum("fsm,sc->fcm", product, place)


def per_device(features, tile_values, tile_rows, tile_cols, tile_counts, weight, cotangent):
    node_count = lax.axis_size("node")
    own_index = lax.axis_index("node")
    slice_width = features.shape[0]
    local_nodes = features.shape[1]
    tile_side = tile_values.shape[1]
    block_count = local_nodes // tile_side

    def pair_of(source):
        return select_pair(tile_values, tile_rows, tile_cols, tile_counts, source)

    totals = jnp.zeros((slice_width, block_count, tile_side), jnp.float32)
    totals = add_forward(totals, features, pair_of(own_index), 1.0)

    def ahead_step(step, carry):
        running, moving = carry
        moving = passed_along(moving, "node", 1)
        source = (own_index - step) % node_count
        return (add_forward(running, moving, pair_of(source), 1.0), moving)

    totals, _ = lax.fori_loop(1, node_count, ahead_step, (totals, features))
    aggregated = totals.reshape(slice_width, local_nodes).astype(jnp.bfloat16)
    full_rows = lax.all_to_all(aggregated, "feat", split_axis=1, concat_axis=0, tiled=True)
    pre = jnp.dot(weight.T, full_rows, preferred_element_type=jnp.float32)
    activated = jax.nn.silu(pre).astype(jnp.bfloat16)
    sigma = jax.nn.sigmoid(pre)
    dpre = (cotangent.astype(jnp.float32) * sigma * (1.0 + pre * (1.0 - sigma))).astype(
        jnp.bfloat16
    )
    weight_part = lax.dot_general(
        full_rows, dpre, (((1,), (1,)), ((), ())), preferred_element_type=jnp.float32
    )
    grad_weight = lax.psum(weight_part, ("node", "feat"))
    dagg = jnp.dot(weight, dpre, preferred_element_type=jnp.float32).astype(jnp.bfloat16)
    grad_slices = lax.all_to_all(dagg, "feat", split_axis=0, concat_axis=1, tiled=True)
    grad_blocks = grad_slices.reshape(slice_width, block_count, tile_side)
    zeros = jnp.zeros((slice_width, block_count, tile_side), jnp.float32)
    start = add_backward(zeros, grad_blocks, pair_of((own_index - 1) % node_count), 1.0)

    def carry_step(step, running):
        running = passed_along(running, "node", 1)
        owner = (own_index - step - 1) % node_count
        return add_backward(running, grad_blocks, pair_of(owner), 1.0)

    gradient = lax.fori_loop(1, node_count, carry_step, start)
    return (activated, grad_weight, gradient.reshape(slice_width, local_nodes))


def solution(mesh):
    placed = (
        P("feat", "node"),
        P("node", None, None),
        P("node", None),
        P("node", None),
        P("node"),
        P(),
        P(None, ("node", "feat")),
    )
    return jax.shard_map(
        per_device,
        mesh=mesh,
        in_specs=placed,
        out_specs=(P(None, ("node", "feat")), P(), P("feat", "node")),
        check_vma=False,
    )
```

profile of v0, /device:TPU:0, one launch (start us, length us, event | category | flops | bytes accessed | tf_op | source)
XLA Modules:
  0.0 227.0 jit_solution(9543807741233657913)
XLA Ops:
  7.2 0.9 copy.98
  8.1 0.7 copy-done.2
  11.7 1.1 fusion.47
  12.9 62.7 %while.32 = (s32[]{:T(128)}, f32[64,4,128]{2,1,0:T(4,128)S(1)}, bf16[64,512]{1,0:T(8,128)(2,1)S(1)}, s32[]{:T(128)}, s32[8,4]{1,0:T(8,128)S(1)}, /*index=5*/s32[...) while((s32[]{:T(128)}, f32[64,4,128]{2,1,0:T(4,128)S(1)}, ...), condition=%wide.region_1.2_spmd, body=%wide.region_0.1_spmd.sunk | while | flops 8945741 | bytes 1245694 | solution.py:67
  12.9 3.0 %collective-permute-start = (bf16[64,512]{1,0:T(8,128)(2,1)S(1)}, bf16[64,512]{1,0:T(8,128)(2,1)S(1)}, u32[]{:S(2)}, u32[]{:S(2)}) collective-permute-start(bf16[64,512]{1,0:T(8,128)(2,1)S(1)} %get-tuple-element.610), channel_id=1, source_target_pairs={{0,4},{4,8},{8,12},{12,16},{16,20},{20,24},{24,28},{28,0},{1,5},{5... | collective-permute-start | bytes 196616 | tf_op jit(solution)/shard_map/while/body/eval_jaxpr/ppermute | solution.py:9
  17.2 4.0 %collective-permute-done = bf16[64,512]{1,0:T(8,128)(2,1)S(1)} collective-permute-done((bf16[64,512]{1,0:T(8,128)(2,1)S(1)}, bf16[64,512]{1,0:T(8,128)(2,1)S(1)}, u32[]{:S(2)}, u32[]{:S(2)}) %collective-permute-start) | collective-permute-done | bytes 65568 | tf_op jit(solution)/shard_map/while/body/eval_jaxpr/ppermute | solution.py:9
  21.5 1.1 fusion.115
  24.3 5.7 %collective-permute-done = bf16[64,512]{1,0:T(8,128)(2,1)S(1)} collective-permute-done((bf16[64,512]{1,0:T(8,128)(2,1)S(1)}, bf16[64,512]{1,0:T(8,128)(2,1)S(1)}, u32[]{:S(2)}, u32[]{:S(2)}) %collective-permute-start) | collective-permute-done | bytes 65568 | tf_op jit(solution)/shard_map/while/body/eval_jaxpr/ppermute | solution.py:9
  30.3 1.1 fusion.115
  33.1 5.7 %collective-permute-done = bf16[64,512]{1,0:T(8,128)(2,1)S(1)} collective-permute-done((bf16[64,512]{1,0:T(8,128)(2,1)S(1)}, bf16[64,512]{1,0:T(8,128)(2,1)S(1)}, u32[]{:S(2)}, u32[]{:S(2)}) %collective-permute-start) | collective-permute-done | bytes 65568 | tf_op jit(solution)/shard_map/while/body/eval_jaxpr/ppermute | solution.py:9
  39.0 1.1 fusion.115
  41.9 5.7 %collective-permute-done = bf16[64,512]{1,0:T(8,128)(2,1)S(1)} collective-permute-done((bf16[64,512]{1,0:T(8,128)(2,1)S(1)}, bf16[64,512]{1,0:T(8,128)(2,1)S(1)}, u32[]{:S(2)}, u32[]{:S(2)}) %collective-permute-start) | collective-permute-done | bytes 65568 | tf_op jit(solution)/shard_map/while/body/eval_jaxpr/ppermute | solution.py:9
  47.8 1.1 fusion.115
  50.6 5.7 %collective-permute-done = bf16[64,512]{1,0:T(8,128)(2,1)S(1)} collective-permute-done((bf16[64,512]{1,0:T(8,128)(2,1)S(1)}, bf16[64,512]{1,0:T(8,128)(2,1)S(1)}, u32[]{:S(2)}, u32[]{:S(2)}) %collective-permute-start) | collective-permute-done | bytes 65568 | tf_op jit(solution)/shard_map/while/body/eval_jaxpr/ppermute | solution.py:9
  56.6 1.1 fusion.115
  59.4 5.7 %collective-permute-done = bf16[64,512]{1,0:T(8,128)(2,1)S(1)} collective-permute-done((bf16[64,512]{1,0:T(8,128)(2,1)S(1)}, bf16[64,512]{1,0:T(8,128)(2,1)S(1)}, u32[]{:S(2)}, u32[]{:S(2)}) %collective-permute-start) | collective-permute-done | bytes 65568 | tf_op jit(solution)/shard_map/while/body/eval_jaxpr/ppermute | solution.py:9
  65.3 1.1 fusion.115
  68.2 5.7 %collective-permute-done = bf16[64,512]{1,0:T(8,128)(2,1)S(1)} collective-permute-done((bf16[64,512]{1,0:T(8,128)(2,1)S(1)}, bf16[64,512]{1,0:T(8,128)(2,1)S(1)}, u32[]{:S(2)}, u32[]{:S(2)}) %collective-permute-start) | collective-permute-done | bytes 65568 | tf_op jit(solution)/shard_map/while/body/eval_jaxpr/ppermute | solution.py:9
  74.1 1.1 fusion.115
  76.2 3.4 %all-to-all-start = ((bf16[64,4,128]{2,0,1:T(8,128)(2,1)}), bf16[64,4,128]{2,0,1:T(8,128)(2,1)S(1)}, u32[]{:S(2)}, u32[]{:S(2)}) async-start(bf16[64,4,128]{2,0,1:T(8,128)(2,1)} %copy.71), calls=%async_computation | async-start | bytes 131072 | tf_op jit(solution)/shard_map/all_to_all | solution.py:69
  79.7 0.7 compare_convert_fusion.2
  80.5 3.3 %all-to-all-done = bf16[64,4,128]{2,0,1:T(8,128)(2,1)S(1)} async-done(((bf16[64,4,128]{2,0,1:T(8,128)(2,1)}), bf16[64,4,128]{2,0,1:T(8,128)(2,1)S(1)}, u32[]{:S(2)}, u32[]{:S(2)}) %all-to-all-start) | async-done | bytes 65568 | tf_op jit(solution)/shard_map/all_to_all | solution.py:69
  84.2 0.7 copy.21
  84.9 3.3 %all-to-all-start.1 = ((bf16[4,64,128]{2,1,0:T(8,128)(2,1)}), bf16[4,64,128]{2,1,0:T(8,128)(2,1)S(1)}, u32[]{:S(2)}, u32[]{:S(2)}) async-start(bf16[4,64,128]{2,1,0:T(8,128)(2,1)} %bitcast.30), calls=%async_computation.1 | async-start | bytes 131072 | tf_op jit(solution)/shard_map/all_to_all | solution.py:81
  88.3 0.9 fusion.77
  89.2 0.7 copy.25
  89.9 2.4 %all-to-all-done.1 = bf16[4,64,128]{2,1,0:T(8,128)(2,1)S(1)} async-done(((bf16[4,64,128]{2,1,0:T(8,128)(2,1)}), bf16[4,64,128]{2,1,0:T(8,128)(2,1)S(1)}, u32[]{:S(2)}, u32[]{:S(2)}) %all-to-all-start.1) | async-done | bytes 65568 | tf_op jit(solution)/shard_map/all_to_all | solution.py:81
  92.6 1.1 fusion.45
  93.9 58.6 %while.33 = (s32[]{:T(128)}, f32[64,4,128]{2,1,0:T(4,128)S(1)}, s32[]{:T(128)}, s32[8,4]{1,0:T(8,128)S(1)}, s32[8]{0:T(128)S(1)}, /*index=5*/bf16[32,128,128]{2,...) while((s32[]{:T(128)}, f32[64,4,128]{2,1,0:T(4,128)S(1)}, ...), condition=%wide.region_4.5_spmd, body=%wide.region_3.4_spmd.sunk | while | flops 8945742 | bytes 1245714 | solution.py:91
  94.2 1.1 fusion.125
  96.5 5.2 %collective-permute-done.1 = f32[64,4,128]{2,1,0:T(4,128)S(1)} collective-permute-done((f32[64,4,128]{2,1,0:T(4,128)S(1)}, f32[64,4,128]{2,1,0:T(4,128)S(1)}, u32[]{:S(2)}, u32[]{:S(2)}) %collective-permute-start.1) | collective-permute-done | bytes 131104 | tf_op jit(solution)/shard_map/while/body/eval_jaxpr/ppermute | solution.py:9
  102.5 1.1 fusion.125
  104.8 5.2 %collective-permute-done.1 = f32[64,4,128]{2,1,0:T(4,128)S(1)} collective-permute-done((f32[64,4,128]{2,1,0:T(4,128)S(1)}, f32[64,4,128]{2,1,0:T(4,128)S(1)}, u32[]{:S(2)}, u32[]{:S(2)}) %collective-permute-start.1) | collective-permute-done | bytes 131104 | tf_op jit(solution)/shard_map/while/body/eval_jaxpr/ppermute | solution.py:9
  110.7 1.1 fusion.125
  112.4 0.6 compare_convert_fusion.7
  113.0 5.2 %collective-permute-done.1 = f32[64,4,128]{2,1,0:T(4,128)S(1)} collective-permute-done((f32[64,4,128]{2,1,0:T(4,128)S(1)}, f32[64,4,128]{2,1,0:T(4,128)S(1)}, u32[]{:S(2)}, u32[]{:S(2)}) %collective-permute-start.1) | collective-permute-done | bytes 131104 | tf_op jit(solution)/shard_map/while/body/eval_jaxpr/ppermute | solution.py:9
  118.9 1.1 fusion.125
  120.6 0.6 compare_convert_fusion.7
  121.2 5.1 %collective-permute-done.1 = f32[64,4,128]{2,1,0:T(4,128)S(1)} collective-permute-done((f32[64,4,128]{2,1,0:T(4,128)S(1)}, f32[64,4,128]{2,1,0:T(4,128)S(1)}, u32[]{:S(2)}, u32[]{:S(2)}) %collective-permute-start.1) | collective-permute-done | bytes 131104 | tf_op jit(solution)/shard_map/while/body/eval_jaxpr/ppermute | solution.py:9
  127.0 1.1 fusion.125
  129.3 5.3 %collective-permute-done.1 = f32[64,4,128]{2,1,0:T(4,128)S(1)} collective-permute-done((f32[64,4,128]{2,1,0:T(4,128)S(1)}, f32[64,4,128]{2,1,0:T(4,128)S(1)}, u32[]{:S(2)}, u32[]{:S(2)}) %collective-permute-start.1) | collective-permute-done | bytes 131104 | tf_op jit(solution)/shard_map/while/body/eval_jaxpr/ppermute | solution.py:9
  135.4 1.1 fusion.125
  137.7 6.3 %collective-permute-done.1 = f32[64,4,128]{2,1,0:T(4,128)S(1)} collective-permute-done((f32[64,4,128]{2,1,0:T(4,128)S(1)}, f32[64,4,128]{2,1,0:T(4,128)S(1)}, u32[]{:S(2)}, u32[]{:S(2)}) %collective-permute-start.1) | collective-permute-done | bytes 131104 | tf_op jit(solution)/shard_map/while/body/eval_jaxpr/ppermute | solution.py:9
  144.7 1.1 fusion.125
  147.0 5.2 %collective-permute-done.1 = f32[64,4,128]{2,1,0:T(4,128)S(1)} collective-permute-done((f32[64,4,128]{2,1,0:T(4,128)S(1)}, f32[64,4,128]{2,1,0:T(4,128)S(1)}, u32[]{:S(2)}, u32[]{:S(2)}) %collective-permute-start.1) | collective-permute-done | bytes 131104 | tf_op jit(solution)/shard_map/while/body/eval_jaxpr/ppermute | solution.py:9
  152.5 0.7 copy.72
  153.2 65.3 %all-reduce.2.cloned.1.call-done = f32[256,256]{1,0:T(8,128)} async-done(((f32[256,256]{1,0:T(8,128)}), f32[256,256]{1,0:T(8,128)}) %all-reduce.2.cloned.1.call-update) | async-done | bytes 262160 | tf_op jit(solution)/shard_map/psum | solution.py:79
  218.5 1.7 copy.99
  (121 shorter events, 30.4 us)
Async XLA Ops:
  7.2 76.6 %copy-start = (bf16[256,256]{1,0:T(8,128)(2,1)S(1)}, bf16[256,256]{1,0:T(8,128)(2,1)}, u32[]{:S(2)}) copy-start(bf16[256,256]{1,0:T(8,128)(2,1)} %param.16) | copy-start | bytes 393220
  8.1 0.7 copy-start.2
  8.7 0.7 copy-start.3
  9.5 0.7 copy-start.4
  12.9 8.3 %collective-permute-start = (bf16[64,512]{1,0:T(8,128)(2,1)S(1)}, bf16[64,512]{1,0:T(8,128)(2,1)S(1)}, u32[]{:S(2)}, u32[]{:S(2)}) collective-permute-start(bf16[64,512]{1,0:T(8,128)(2,1)S(1)} %get-tuple-element.610), channel_id=1, source_target_pairs={{0,4},{4,8},{8,12},{12,16},{16,20},{20,24},{24,28},{28,0},{1,5},{5... | collective-permute-start | bytes 196616 | tf_op jit(solution)/shard_map/while/body/eval_jaxpr/ppermute | solution.py:9
  23.0 7.0 %collective-permute-start = (bf16[64,512]{1,0:T(8,128)(2,1)S(1)}, bf16[64,512]{1,0:T(8,128)(2,1)S(1)}, u32[]{:S(2)}, u32[]{:S(2)}) collective-permute-start(bf16[64,512]{1,0:T(8,128)(2,1)S(1)} %get-tuple-element.610), channel_id=1, source_target_pairs={{0,4},{4,8},{8,12},{12,16},{16,20},{20,24},{24,28},{28,0},{1,5},{5... | collective-permute-start | bytes 196616 | tf_op jit(solution)/shard_map/while/body/eval_jaxpr/ppermute | solution.py:9
  31.7 7.0 %collective-permute-start = (bf16[64,512]{1,0:T(8,128)(2,1)S(1)}, bf16[64,512]{1,0:T(8,128)(2,1)S(1)}, u32[]{:S(2)}, u32[]{:S(2)}) collective-permute-start(bf16[64,512]{1,0:T(8,128)(2,1)S(1)} %get-tuple-element.610), channel_id=1, source_target_pairs={{0,4},{4,8},{8,12},{12,16},{16,20},{20,24},{24,28},{28,0},{1,5},{5... | collective-permute-start | bytes 196616 | tf_op jit(solution)/shard_map/while/body/eval_jaxpr/ppermute | solution.py:9
  40.5 7.0 %collective-permute-start = (bf16[64,512]{1,0:T(8,128)(2,1)S(1)}, bf16[64,512]{1,0:T(8,128)(2,1)S(1)}, u32[]{:S(2)}, u32[]{:S(2)}) collective-permute-start(bf16[64,512]{1,0:T(8,128)(2,1)S(1)} %get-tuple-element.610), channel_id=1, source_target_pairs={{0,4},{4,8},{8,12},{12,16},{16,20},{20,24},{24,28},{28,0},{1,5},{5... | collective-permute-start | bytes 196616 | tf_op jit(solution)/shard_map/while/body/eval_jaxpr/ppermute | solution.py:9
  49.3 7.0 %collective-permute-start = (bf16[64,512]{1,0:T(8,128)(2,1)S(1)}, bf16[64,512]{1,0:T(8,128)(2,1)S(1)}, u32[]{:S(2)}, u32[]{:S(2)}) collective-permute-start(bf16[64,512]{1,0:T(8,128)(2,1)S(1)} %get-tuple-element.610), channel_id=1, source_target_pairs={{0,4},{4,8},{8,12},{12,16},{16,20},{20,24},{24,28},{28,0},{1,5},{5... | collective-permute-start | bytes 196616 | tf_op jit(solution)/shard_map/while/body/eval_jaxpr/ppermute | solution.py:9
  58.1 7.0 %collective-permute-start = (bf16[64,512]{1,0:T(8,128)(2,1)S(1)}, bf16[64,512]{1,0:T(8,128)(2,1)S(1)}, u32[]{:S(2)}, u32[]{:S(2)}) collective-permute-start(bf16[64,512]{1,0:T(8,128)(2,1)S(1)} %get-tuple-element.610), channel_id=1, source_target_pairs={{0,4},{4,8},{8,12},{12,16},{16,20},{20,24},{24,28},{28,0},{1,5},{5... | collective-permute-start | bytes 196616 | tf_op jit(solution)/shard_map/while/body/eval_jaxpr/ppermute | solution.py:9
  66.8 7.0 %collective-permute-start = (bf16[64,512]{1,0:T(8,128)(2,1)S(1)}, bf16[64,512]{1,0:T(8,128)(2,1)S(1)}, u32[]{:S(2)}, u32[]{:S(2)}) collective-permute-start(bf16[64,512]{1,0:T(8,128)(2,1)S(1)} %get-tuple-element.610), channel_id=1, source_target_pairs={{0,4},{4,8},{8,12},{12,16},{16,20},{20,24},{24,28},{28,0},{1,5},{5... | collective-permute-start | bytes 196616 | tf_op jit(solution)/shard_map/while/body/eval_jaxpr/ppermute | solution.py:9
  76.2 4.1 %copy-start.1 = (bf16[256,128]{1,0:T(8,128)(2,1)S(1)}, bf16[256,128]{1,0:T(8,128)(2,1)}, u32[]{:S(2)}) copy-start(bf16[256,128]{1,0:T(8,128)(2,1)} %param.17) | copy-start | bytes 196612
  76.2 7.5 %all-to-all-start = ((bf16[64,4,128]{2,0,1:T(8,128)(2,1)}), bf16[64,4,128]{2,0,1:T(8,128)(2,1)S(1)}, u32[]{:S(2)}, u32[]{:S(2)}) async-start(bf16[64,4,128]{2,0,1:T(8,128)(2,1)} %copy.71), calls=%async_computation | async-start | bytes 131072 | tf_op jit(solution)/shard_map/all_to_all | solution.py:69
  84.9 7.4 %all-to-all-start.1 = ((bf16[4,64,128]{2,1,0:T(8,128)(2,1)}), bf16[4,64,128]{2,1,0:T(8,128)(2,1)S(1)}, u32[]{:S(2)}, u32[]{:S(2)}) async-start(bf16[4,64,128]{2,1,0:T(8,128)(2,1)} %bitcast.30), calls=%async_computation.1 | async-start | bytes 131072 | tf_op jit(solution)/shard_map/all_to_all | solution.py:81
  88.2 130.3 %all-reduce.2.cloned.1.call-start = ((), (), s32[]{:S(2)}) async-start(), calls=%async_computation.2 | async-start | bytes 524288 | tf_op jit(solution)/shard_map/psum | solution.py:79
  93.9 7.9 %collective-permute-start.1 = (f32[64,4,128]{2,1,0:T(4,128)S(1)}, f32[64,4,128]{2,1,0:T(4,128)S(1)}, u32[]{:S(2)}, u32[]{:S(2)}) collective-permute-start(f32[64,4,128]{2,1,0:T(4,128)S(1)} %get-tuple-element.652), channel_id=1, source_target_pairs={{0,4},{4,8},{8,12},{12,16},{16,20},{20,24},{24,28},{28,0},{1,5},{5... | collective-permute-start | bytes 393224 | tf_op jit(solution)/shard_map/while/body/eval_jaxpr/ppermute | solution.py:9
  102.1 7.9 %collective-permute-start.1 = (f32[64,4,128]{2,1,0:T(4,128)S(1)}, f32[64,4,128]{2,1,0:T(4,128)S(1)}, u32[]{:S(2)}, u32[]{:S(2)}) collective-permute-start(f32[64,4,128]{2,1,0:T(4,128)S(1)} %get-tuple-element.652), channel_id=1, source_target_pairs={{0,4},{4,8},{8,12},{12,16},{16,20},{20,24},{24,28},{28,0},{1,5},{5... | collective-permute-start | bytes 393224 | tf_op jit(solution)/shard_map/while/body/eval_jaxpr/ppermute | solution.py:9
  110.4 7.9 %collective-permute-start.1 = (f32[64,4,128]{2,1,0:T(4,128)S(1)}, f32[64,4,128]{2,1,0:T(4,128)S(1)}, u32[]{:S(2)}, u32[]{:S(2)}) collective-permute-start(f32[64,4,128]{2,1,0:T(4,128)S(1)} %get-tuple-element.652), channel_id=1, source_target_pairs={{0,4},{4,8},{8,12},{12,16},{16,20},{20,24},{24,28},{28,0},{1,5},{5... | collective-permute-start | bytes 393224 | tf_op jit(solution)/shard_map/while/body/eval_jaxpr/ppermute | solution.py:9
  118.6 7.7 %collective-permute-start.1 = (f32[64,4,128]{2,1,0:T(4,128)S(1)}, f32[64,4,128]{2,1,0:T(4,128)S(1)}, u32[]{:S(2)}, u32[]{:S(2)}) collective-permute-start(f32[64,4,128]{2,1,0:T(4,128)S(1)} %get-tuple-element.652), channel_id=1, source_target_pairs={{0,4},{4,8},{8,12},{12,16},{16,20},{20,24},{24,28},{28,0},{1,5},{5... | collective-permute-start | bytes 393224 | tf_op jit(solution)/shard_map/while/body/eval_jaxpr/ppermute | solution.py:9
  126.7 8.0 %collective-permute-start.1 = (f32[64,4,128]{2,1,0:T(4,128)S(1)}, f32[64,4,128]{2,1,0:T(4,128)S(1)}, u32[]{:S(2)}, u32[]{:S(2)}) collective-permute-start(f32[64,4,128]{2,1,0:T(4,128)S(1)} %get-tuple-element.652), channel_id=1, source_target_pairs={{0,4},{4,8},{8,12},{12,16},{16,20},{20,24},{24,28},{28,0},{1,5},{5... | collective-permute-start | bytes 393224 | tf_op jit(solution)/shard_map/while/body/eval_jaxpr/ppermute | solution.py:9
  135.0 8.9 %collective-permute-start.1 = (f32[64,4,128]{2,1,0:T(4,128)S(1)}, f32[64,4,128]{2,1,0:T(4,128)S(1)}, u32[]{:S(2)}, u32[]{:S(2)}) collective-permute-start(f32[64,4,128]{2,1,0:T(4,128)S(1)} %get-tuple-element.652), channel_id=1, source_target_pairs={{0,4},{4,8},{8,12},{12,16},{16,20},{20,24},{24,28},{28,0},{1,5},{5... | collective-permute-start | bytes 393224 | tf_op jit(solution)/shard_map/while/body/eval_jaxpr/ppermute | solution.py:9
  144.3 7.8 %collective-permute-start.1 = (f32[64,4,128]{2,1,0:T(4,128)S(1)}, f32[64,4,128]{2,1,0:T(4,128)S(1)}, u32[]{:S(2)}, u32[]{:S(2)}) collective-permute-start(f32[64,4,128]{2,1,0:T(4,128)S(1)} %get-tuple-element.652), channel_id=1, source_target_pairs={{0,4},{4,8},{8,12},{12,16},{16,20},{20,24},{24,28},{28,0},{1,5},{5... | collective-permute-start | bytes 393224 | tf_op jit(solution)/shard_map/while/body/eval_jaxpr/ppermute | solution.py:9
Sparse Core Ops, SparseCore 0:
  95.1 123.3 all-reduce.1
where the time goes:
time: 228 us; the launch traced here: 227 us
  waiting for transfers between devices  147 us (64%)
  matrix products  27.7 us (12%)
  local copies, waits for them, and re-layouts  16.8 us (7%)
  between operations  14.2 us (6%)
  starting transfers between devices  10.5 us (5%)
  other arithmetic  10.4 us (5%)
    ppermute x14, waiting for transfers between devices, passed_along(): return lax.ppermute(x, axis, [(i, (i + by) % count) for i in range(count)])  75.5 us
    psum x1, waiting for transfers between devices, per_device(): grad_weight = lax.psum(weight_part, ('node', 'feat'))  65.3 us
    convert_element_type x16, other arithmetic, select_pair(): live = (jnp.arange(slots) < number).astype(jnp.float32)  10.4 us
    dynamic_slice x15, local copies, waits for them, and re-layouts, select_pair(): number = lax.dynamic_index_in_dim(tile_counts, source, 0, keepdims=False)  8.87 us
    dot_general x8, matrix products, add_forward(): jnp.einsum('fsm,sjm->fsj', chosen, values, preferred_element_type=jnp.flo...  8.64 us
    dot_general x8, matrix products, add_backward(): jnp.einsum('fsj,sjm->fsm', chosen, values, preferred_element_type=jnp.flo...  8.47 us
    unnamed x15, local copies, waits for them, and re-layouts  5.78 us
  transfers between devices with their start and end apart: 17, of which 17 were waited for; matrix products, arithmetic and copies ran while one was open for 15% of the time, Pallas kernels for 0%

commit v1 on v0

--- a/solution.py
+++ b/solution.py
@@ -2,6 +2,17 @@
 import jax.numpy as jnp
 from jax import lax
 from jax.sharding import PartitionSpec as P
+
+
+def split_up(value, dim, count):
+    before, after = (value.shape[:dim], value.shape[dim + 1 :])
+    return jnp.moveaxis(value.reshape(*before, count, -1, *after), dim, 0)
+
+
+def laid_out(parts, dim):
+    shape = list(parts.shape[1:])
+    shape[dim] *= parts.shape[0]
+    return jnp.moveaxis(parts, 0, dim).reshape(shape)
 
 
 def passed_along(x, axis, by):
@@ -78,7 +89,14 @@
     )
     grad_weight = lax.psum(weight_part, ("node", "feat"))
     dagg = jnp.dot(weight, dpre, preferred_element_type=jnp.float32).astype(jnp.bfloat16)
-    grad_slices = lax.all_to_all(dagg, "feat", split_axis=0, concat_axis=1, tiled=True)
+    size, here = (lax.axis_size("feat"), lax.axis_index("feat"))
+    blocks = split_up(dagg, 0, size)
+    gathered = [blocks[here]]
+    for step_2 in range(1, size):
+        sent = blocks[here ^ step_2]
+        gathered.append(lax.ppermute(sent, "feat", [(i_2, i_2 ^ step_2) for i_2 in range(size)]))
+    blocks = jnp.stack(gathered)[here ^ jnp.arange(size)]
+    grad_slices = laid_out(blocks, 1)
     grad_blocks = grad_slices.reshape(slice_width, block_count, tile_side)
     zeros = jnp.zeros((slice_width, block_count, tile_side), jnp.float32)
     start = add_backward(zeros, grad_blocks, pair_of((own_index - 1) % node_count), 1.0)

time: 228 us -> 220 us (0.965)
  waiting for transfers between devices: 147 us -> 139 us
    psum x1, waiting for transfers between devices: 65.3 us -> 60.2 us  [per_device(): grad_weight = lax.psum(weight_part, ('node', 'feat'))]
    all_to_all x1 -> x0, starting transfers between devices: 3.28 us -> none  [per_device(): lax.all_to_all(dagg, 'feat', split_axis=0, concat_axis=1, tiled=True)]
    all_to_all x1 -> x0, waiting for transfers between devices: 2.4 us -> none  [per_device(): lax.all_to_all(dagg, 'feat', split_axis=0, concat_axis=1, tiled=True)]
  transfers between devices with their start and end apart: 17 -> 19, of which waited for: 17 -> 17; matrix products, arithmetic and copies ran while one was open for 15% -> 16% of each run, Pallas kernels for 0% -> 0%
where the time goes in v1:
time: 220 us; the launch traced here: 219 us
  waiting for transfers between devices  139 us (63%)
  matrix products  27.7 us (13%)
  local copies, waits for them, and re-layouts  17.3 us (8%)
  between operations  14.3 us (6%)
  other arithmetic  10.5 us (5%)
  starting transfers between devices  9.13 us (4%)
    ppermute x14, waiting for transfers between devices, passed_along(): return lax.ppermute(x, axis, [(i, (i + by) % count) for i in range(count)])  75.1 us
    psum x1, waiting for transfers between devices, per_device(): grad_weight = lax.psum(weight_part, ('node', 'feat'))  60.2 us
    convert_element_type x16, other arithmetic, select_pair(): live = (jnp.arange(slots) < number).astype(jnp.float32)  10.5 us
    dynamic_slice x15, local copies, waits for them, and re-layouts, select_pair(): number = lax.dynamic_index_in_dim(tile_counts, source, 0, keepdims=False)  9.49 us
    dot_general x8, matrix products, add_forward(): jnp.einsum('fsm,sjm->fsj', chosen, values, preferred_element_type=jnp.flo...  8.63 us
    dot_general x8, matrix products, add_backward(): jnp.einsum('fsj,sjm->fsm', chosen, values, preferred_element_type=jnp.flo...  8.48 us
    unnamed x15, local copies, waits for them, and re-layouts  5.78 us
  transfers between devices with their start and end apart: 19, of which 17 were waited for; matrix products, arithmetic and copies ran while one was open for 16% of the time, Pallas kernels for 0%

profile of v1, /device:TPU:0, one launch (start us, length us, event | category | flops | bytes accessed | tf_op | source)
XLA Modules:
  0.0 218.8 jit_solution(77976731636377869)
XLA Ops:
  7.2 0.9 copy.97
  10.8 0.7 compare_convert_fusion.3
  11.8 1.1 fusion.47
  13.0 62.7 %while.32 = (s32[]{:T(128)}, f32[64,4,128]{2,1,0:T(4,128)S(1)}, bf16[64,512]{1,0:T(8,128)(2,1)S(1)}, s32[]{:T(128)}, s32[8,4]{1,0:T(8,128)S(1)}, /*index=5*/s32[...) while((s32[]{:T(128)}, f32[64,4,128]{2,1,0:T(4,128)S(1)}, ...), condition=%wide.region_1.2_spmd, body=%wide.region_0.1_spmd.sunk | while | flops 8945741 | bytes 1245694 | solution.py:78
  13.1 3.0 %collective-permute-start = (bf16[64,512]{1,0:T(8,128)(2,1)S(1)}, bf16[64,512]{1,0:T(8,128)(2,1)S(1)}, u32[]{:S(2)}, u32[]{:S(2)}) collective-permute-start(bf16[64,512]{1,0:T(8,128)(2,1)S(1)} %get-tuple-element.614), channel_id=1, source_target_pairs={{0,4},{4,8},{8,12},{12,16},{16,20},{20,24},{24,28},{28,0},{1,5},{5... | collective-permute-start | bytes 196616 | tf_op jit(solution)/shard_map/while/body/eval_jaxpr/ppermute | solution.py:20
  16.7 0.7 compare_convert_fusion.6
  17.4 3.9 %collective-permute-done = bf16[64,512]{1,0:T(8,128)(2,1)S(1)} collective-permute-done((bf16[64,512]{1,0:T(8,128)(2,1)S(1)}, bf16[64,512]{1,0:T(8,128)(2,1)S(1)}, u32[]{:S(2)}, u32[]{:S(2)}) %collective-permute-start) | collective-permute-done | bytes 65568 | tf_op jit(solution)/shard_map/while/body/eval_jaxpr/ppermute | solution.py:20
  21.6 1.1 fusion.120
  23.8 0.7 compare_convert_fusion.6
  24.5 5.6 %collective-permute-done = bf16[64,512]{1,0:T(8,128)(2,1)S(1)} collective-permute-done((bf16[64,512]{1,0:T(8,128)(2,1)S(1)}, bf16[64,512]{1,0:T(8,128)(2,1)S(1)}, u32[]{:S(2)}, u32[]{:S(2)}) %collective-permute-start) | collective-permute-done | bytes 65568 | tf_op jit(solution)/shard_map/while/body/eval_jaxpr/ppermute | solution.py:20
  30.4 1.1 fusion.120
  32.6 0.7 compare_convert_fusion.6
  33.3 5.6 %collective-permute-done = bf16[64,512]{1,0:T(8,128)(2,1)S(1)} collective-permute-done((bf16[64,512]{1,0:T(8,128)(2,1)S(1)}, bf16[64,512]{1,0:T(8,128)(2,1)S(1)}, u32[]{:S(2)}, u32[]{:S(2)}) %collective-permute-start) | collective-permute-done | bytes 65568 | tf_op jit(solution)/shard_map/while/body/eval_jaxpr/ppermute | solution.py:20
  39.1 1.1 fusion.120
  41.4 0.7 compare_convert_fusion.6
  42.1 5.6 %collective-permute-done = bf16[64,512]{1,0:T(8,128)(2,1)S(1)} collective-permute-done((bf16[64,512]{1,0:T(8,128)(2,1)S(1)}, bf16[64,512]{1,0:T(8,128)(2,1)S(1)}, u32[]{:S(2)}, u32[]{:S(2)}) %collective-permute-start) | collective-permute-done | bytes 65568 | tf_op jit(solution)/shard_map/while/body/eval_jaxpr/ppermute | solution.py:20
  47.9 1.1 fusion.120
  50.2 0.7 compare_convert_fusion.6
  50.8 5.6 %collective-permute-done = bf16[64,512]{1,0:T(8,128)(2,1)S(1)} collective-permute-done((bf16[64,512]{1,0:T(8,128)(2,1)S(1)}, bf16[64,512]{1,0:T(8,128)(2,1)S(1)}, u32[]{:S(2)}, u32[]{:S(2)}) %collective-permute-start) | collective-permute-done | bytes 65568 | tf_op jit(solution)/shard_map/while/body/eval_jaxpr/ppermute | solution.py:20
  56.7 1.1 fusion.120
  58.9 0.7 compare_convert_fusion.6
  59.6 5.6 %collective-permute-done = bf16[64,512]{1,0:T(8,128)(2,1)S(1)} collective-permute-done((bf16[64,512]{1,0:T(8,128)(2,1)S(1)}, bf16[64,512]{1,0:T(8,128)(2,1)S(1)}, u32[]{:S(2)}, u32[]{:S(2)}) %collective-permute-start) | collective-permute-done | bytes 65568 | tf_op jit(solution)/shard_map/while/body/eval_jaxpr/ppermute | solution.py:20
  65.4 1.1 fusion.120
  68.4 5.6 %collective-permute-done = bf16[64,512]{1,0:T(8,128)(2,1)S(1)} collective-permute-done((bf16[64,512]{1,0:T(8,128)(2,1)S(1)}, bf16[64,512]{1,0:T(8,128)(2,1)S(1)}, u32[]{:S(2)}, u32[]{:S(2)}) %collective-permute-start) | collective-permute-done | bytes 65568 | tf_op jit(solution)/shard_map/while/body/eval_jaxpr/ppermute | solution.py:20
  74.2 1.1 fusion.120
  76.3 3.4 %all-to-all-start = ((bf16[64,4,128]{2,0,1:T(8,128)(2,1)}), bf16[64,4,128]{2,0,1:T(8,128)(2,1)S(1)}, u32[]{:S(2)}, u32[]{:S(2)}) async-start(bf16[64,4,128]{2,0,1:T(8,128)(2,1)} %copy.70), calls=%async_computation | async-start | bytes 131072 | tf_op jit(solution)/shard_map/all_to_all | solution.py:80
  80.7 3.2 %all-to-all-done = bf16[64,4,128]{2,0,1:T(8,128)(2,1)S(1)} async-done(((bf16[64,4,128]{2,0,1:T(8,128)(2,1)}), bf16[64,4,128]{2,0,1:T(8,128)(2,1)S(1)}, u32[]{:S(2)}, u32[]{:S(2)}) %all-to-all-start) | async-done | bytes 65568 | tf_op jit(solution)/shard_map/all_to_all | solution.py:80
  84.5 1.3 collective-permute-start.3
  86.4 0.9 fusion.82
  87.3 0.7 copy.24
  89.2 1.1 fusion.45
  90.5 58.9 %while.33 = (s32[]{:T(128)}, f32[64,4,128]{2,1,0:T(4,128)S(1)}, s32[]{:T(128)}, s32[8,4]{1,0:T(8,128)S(1)}, s32[8]{0:T(128)S(1)}, /*index=5*/bf16[32,128,128]{2,...) while((s32[]{:T(128)}, f32[64,4,128]{2,1,0:T(4,128)S(1)}, ...), condition=%wide.region_4.5_spmd, body=%wide.region_3.4_spmd.sunk | while | flops 8945742 | bytes 1245714 | solution.py:109
  90.8 1.1 fusion.130
  93.1 5.4 %collective-permute-done.1 = f32[64,4,128]{2,1,0:T(4,128)S(1)} collective-permute-done((f32[64,4,128]{2,1,0:T(4,128)S(1)}, f32[64,4,128]{2,1,0:T(4,128)S(1)}, u32[]{:S(2)}, u32[]{:S(2)}) %collective-permute-start.1) | collective-permute-done | bytes 131104 | tf_op jit(solution)/shard_map/while/body/eval_jaxpr/ppermute | solution.py:20
  99.2 1.1 fusion.130
  101.5 5.2 %collective-permute-done.1 = f32[64,4,128]{2,1,0:T(4,128)S(1)} collective-permute-done((f32[64,4,128]{2,1,0:T(4,128)S(1)}, f32[64,4,128]{2,1,0:T(4,128)S(1)}, u32[]{:S(2)}, u32[]{:S(2)}) %collective-permute-start.1) | collective-permute-done | bytes 131104 | tf_op jit(solution)/shard_map/while/body/eval_jaxpr/ppermute | solution.py:20
  107.4 1.1 fusion.130
  109.7 5.1 %collective-permute-done.1 = f32[64,4,128]{2,1,0:T(4,128)S(1)} collective-permute-done((f32[64,4,128]{2,1,0:T(4,128)S(1)}, f32[64,4,128]{2,1,0:T(4,128)S(1)}, u32[]{:S(2)}, u32[]{:S(2)}) %collective-permute-start.1) | collective-permute-done | bytes 131104 | tf_op jit(solution)/shard_map/while/body/eval_jaxpr/ppermute | solution.py:20
  115.6 1.1 fusion.130
  117.9 5.2 %collective-permute-done.1 = f32[64,4,128]{2,1,0:T(4,128)S(1)} collective-permute-done((f32[64,4,128]{2,1,0:T(4,128)S(1)}, f32[64,4,128]{2,1,0:T(4,128)S(1)}, u32[]{:S(2)}, u32[]{:S(2)}) %collective-permute-start.1) | collective-permute-done | bytes 131104 | tf_op jit(solution)/shard_map/while/body/eval_jaxpr/ppermute | solution.py:20
  123.7 1.1 fusion.130
  126.0 5.3 %collective-permute-done.1 = f32[64,4,128]{2,1,0:T(4,128)S(1)} collective-permute-done((f32[64,4,128]{2,1,0:T(4,128)S(1)}, f32[64,4,128]{2,1,0:T(4,128)S(1)}, u32[]{:S(2)}, u32[]{:S(2)}) %collective-permute-start.1) | collective-permute-done | bytes 131104 | tf_op jit(solution)/shard_map/while/body/eval_jaxpr/ppermute | solution.py:20
  132.1 1.1 fusion.130
  134.4 6.5 %collective-permute-done.1 = f32[64,4,128]{2,1,0:T(4,128)S(1)} collective-permute-done((f32[64,4,128]{2,1,0:T(4,128)S(1)}, f32[64,4,128]{2,1,0:T(4,128)S(1)}, u32[]{:S(2)}, u32[]{:S(2)}) %collective-permute-start.1) | collective-permute-done | bytes 131104 | tf_op jit(solution)/shard_map/while/body/eval_jaxpr/ppermute | solution.py:20
  141.7 1.1 fusion.130
  144.0 5.1 %collective-permute-done.1 = f32[64,4,128]{2,1,0:T(4,128)S(1)} collective-permute-done((f32[64,4,128]{2,1,0:T(4,128)S(1)}, f32[64,4,128]{2,1,0:T(4,128)S(1)}, u32[]{:S(2)}, u32[]{:S(2)}) %collective-permute-start.1) | collective-permute-done | bytes 131104 | tf_op jit(solution)/shard_map/while/body/eval_jaxpr/ppermute | solution.py:20
  150.1 60.2 %all-reduce.2.cloned.1.call-done = f32[256,256]{1,0:T(8,128)} async-done(((f32[256,256]{1,0:T(8,128)}), f32[256,256]{1,0:T(8,128)}) %all-reduce.2.cloned.1.call-update) | async-done | bytes 262160 | tf_op jit(solution)/shard_map/psum | solution.py:90
  210.3 1.7 copy.98
  (130 shorter events, 31.3 us)
Async XLA Ops:
  7.2 76.7 %copy-start = (bf16[256,256]{1,0:T(8,128)(2,1)S(1)}, bf16[256,256]{1,0:T(8,128)(2,1)}, u32[]{:S(2)}) copy-start(bf16[256,256]{1,0:T(8,128)(2,1)} %param.16) | copy-start | bytes 393220
  8.1 0.7 copy-start.3
  8.7 0.7 copy-start.2
  9.5 0.7 copy-start.4
  13.1 8.3 %collective-permute-start = (bf16[64,512]{1,0:T(8,128)(2,1)S(1)}, bf16[64,512]{1,0:T(8,128)(2,1)S(1)}, u32[]{:S(2)}, u32[]{:S(2)}) collective-permute-start(bf16[64,512]{1,0:T(8,128)(2,1)S(1)} %get-tuple-element.614), channel_id=1, source_target_pairs={{0,4},{4,8},{8,12},{12,16},{16,20},{20,24},{24,28},{28,0},{1,5},{5... | collective-permute-start | bytes 196616 | tf_op jit(solution)/shard_map/while/body/eval_jaxpr/ppermute | solution.py:20
  23.1 7.0 %collective-permute-start = (bf16[64,512]{1,0:T(8,128)(2,1)S(1)}, bf16[64,512]{1,0:T(8,128)(2,1)S(1)}, u32[]{:S(2)}, u32[]{:S(2)}) collective-permute-start(bf16[64,512]{1,0:T(8,128)(2,1)S(1)} %get-tuple-element.614), channel_id=1, source_target_pairs={{0,4},{4,8},{8,12},{12,16},{16,20},{20,24},{24,28},{28,0},{1,5},{5... | collective-permute-start | bytes 196616 | tf_op jit(solution)/shard_map/while/body/eval_jaxpr/ppermute | solution.py:20
  31.9 7.0 %collective-permute-start = (bf16[64,512]{1,0:T(8,128)(2,1)S(1)}, bf16[64,512]{1,0:T(8,128)(2,1)S(1)}, u32[]{:S(2)}, u32[]{:S(2)}) collective-permute-start(bf16[64,512]{1,0:T(8,128)(2,1)S(1)} %get-tuple-element.614), channel_id=1, source_target_pairs={{0,4},{4,8},{8,12},{12,16},{16,20},{20,24},{24,28},{28,0},{1,5},{5... | collective-permute-start | bytes 196616 | tf_op jit(solution)/shard_map/while/body/eval_jaxpr/ppermute | solution.py:20
  40.6 7.0 %collective-permute-start = (bf16[64,512]{1,0:T(8,128)(2,1)S(1)}, bf16[64,512]{1,0:T(8,128)(2,1)S(1)}, u32[]{:S(2)}, u32[]{:S(2)}) collective-permute-start(bf16[64,512]{1,0:T(8,128)(2,1)S(1)} %get-tuple-element.614), channel_id=1, source_target_pairs={{0,4},{4,8},{8,12},{12,16},{16,20},{20,24},{24,28},{28,0},{1,5},{5... | collective-permute-start | bytes 196616 | tf_op jit(solution)/shard_map/while/body/eval_jaxpr/ppermute | solution.py:20
  49.4 7.0 %collective-permute-start = (bf16[64,512]{1,0:T(8,128)(2,1)S(1)}, bf16[64,512]{1,0:T(8,128)(2,1)S(1)}, u32[]{:S(2)}, u32[]{:S(2)}) collective-permute-start(bf16[64,512]{1,0:T(8,128)(2,1)S(1)} %get-tuple-element.614), channel_id=1, source_target_pairs={{0,4},{4,8},{8,12},{12,16},{16,20},{20,24},{24,28},{28,0},{1,5},{5... | collective-permute-start | bytes 196616 | tf_op jit(solution)/shard_map/while/body/eval_jaxpr/ppermute | solution.py:20
  58.2 7.0 %collective-permute-start = (bf16[64,512]{1,0:T(8,128)(2,1)S(1)}, bf16[64,512]{1,0:T(8,128)(2,1)S(1)}, u32[]{:S(2)}, u32[]{:S(2)}) collective-permute-start(bf16[64,512]{1,0:T(8,128)(2,1)S(1)} %get-tuple-element.614), channel_id=1, source_target_pairs={{0,4},{4,8},{8,12},{12,16},{16,20},{20,24},{24,28},{28,0},{1,5},{5... | collective-permute-start | bytes 196616 | tf_op jit(solution)/shard_map/while/body/eval_jaxpr/ppermute | solution.py:20
  66.9 7.0 %collective-permute-start = (bf16[64,512]{1,0:T(8,128)(2,1)S(1)}, bf16[64,512]{1,0:T(8,128)(2,1)S(1)}, u32[]{:S(2)}, u32[]{:S(2)}) collective-permute-start(bf16[64,512]{1,0:T(8,128)(2,1)S(1)} %get-tuple-element.614), channel_id=1, source_target_pairs={{0,4},{4,8},{8,12},{12,16},{16,20},{20,24},{24,28},{28,0},{1,5},{5... | collective-permute-start | bytes 196616 | tf_op jit(solution)/shard_map/while/body/eval_jaxpr/ppermute | solution.py:20
  76.3 4.2 %copy-start.1 = (bf16[256,128]{1,0:T(8,128)(2,1)S(1)}, bf16[256,128]{1,0:T(8,128)(2,1)}, u32[]{:S(2)}) copy-start(bf16[256,128]{1,0:T(8,128)(2,1)} %param.17) | copy-start | bytes 196612
  76.3 7.5 %all-to-all-start = ((bf16[64,4,128]{2,0,1:T(8,128)(2,1)}), bf16[64,4,128]{2,0,1:T(8,128)(2,1)S(1)}, u32[]{:S(2)}, u32[]{:S(2)}) async-start(bf16[64,4,128]{2,0,1:T(8,128)(2,1)} %copy.70), calls=%async_computation | async-start | bytes 131072 | tf_op jit(solution)/shard_map/all_to_all | solution.py:80
  79.8 130.5 %all-reduce.2.cloned.1.call-start = ((), (), s32[]{:S(2)}) async-start(), calls=%async_computation.1 | async-start | bytes 524288 | tf_op jit(solution)/shard_map/psum | solution.py:90
  84.4 3.6 %collective-permute-start.4 = (bf16[64,128]{1,0:T(8,128)(2,1)S(1)}, bf16[64,128]{1,0:T(8,128)(2,1)S(1)}, u32[]{:S(2)}, u32[]{:S(2)}) collective-permute-start(bf16[64,128]{1,0:T(8,128)(2,1)S(1)} %get-tuple-element.485), channel_id=1, source_target_pairs={{0,3},{1,2},{2,1},{3,0},{4,7},{5,6},{6,5},{7,4},{8,11},{9,10},{10,... | collective-permute-start | bytes 49160 | tf_op jit(solution)/shard_map/ppermute | solution.py:97
  84.5 3.8 %collective-permute-start.3 = (bf16[64,128]{1,0:T(8,128)(2,1)S(1)}, bf16[64,128]{1,0:T(8,128)(2,1)S(1)}, u32[]{:S(2)}, u32[]{:S(2)}) collective-permute-start(bf16[64,128]{1,0:T(8,128)(2,1)S(1)} %get-tuple-element.486), channel_id=1, source_target_pairs={{0,2},{1,3},{2,0},{3,1},{4,6},{5,7},{6,4},{7,5},{8,10},{9,11},{10,... | collective-permute-start | bytes 49160 | tf_op jit(solution)/shard_map/ppermute | solution.py:97
  85.8 2.5 %collective-permute-start.2 = (bf16[64,128]{1,0:T(8,128)(2,1)S(1)}, bf16[64,128]{1,0:T(8,128)(2,1)S(1)}, u32[]{:S(2)}, u32[]{:S(2)}) collective-permute-start(bf16[64,128]{1,0:T(8,128)(2,1)S(1)} %get-tuple-element.487), channel_id=1, source_target_pairs={{0,1},{1,0},{2,3},{3,2},{4,5},{5,4},{6,7},{7,6},{8,9},{9,8},{10,11... | collective-permute-start | bytes 49160 | tf_op jit(solution)/shard_map/ppermute | solution.py:97
  90.5 8.0 %collective-permute-start.1 = (f32[64,4,128]{2,1,0:T(4,128)S(1)}, f32[64,4,128]{2,1,0:T(4,128)S(1)}, u32[]{:S(2)}, u32[]{:S(2)}) collective-permute-start(f32[64,4,128]{2,1,0:T(4,128)S(1)} %get-tuple-element.656), channel_id=1, source_target_pairs={{0,4},{4,8},{8,12},{12,16},{16,20},{20,24},{24,28},{28,0},{1,5},{5... | collective-permute-start | bytes 393224 | tf_op jit(solution)/shard_map/while/body/eval_jaxpr/ppermute | solution.py:20
  98.8 7.9 %collective-permute-start.1 = (f32[64,4,128]{2,1,0:T(4,128)S(1)}, f32[64,4,128]{2,1,0:T(4,128)S(1)}, u32[]{:S(2)}, u32[]{:S(2)}) collective-permute-start(f32[64,4,128]{2,1,0:T(4,128)S(1)} %get-tuple-element.656), channel_id=1, source_target_pairs={{0,4},{4,8},{8,12},{12,16},{16,20},{20,24},{24,28},{28,0},{1,5},{5... | collective-permute-start | bytes 393224 | tf_op jit(solution)/shard_map/while/body/eval_jaxpr/ppermute | solution.py:20
  107.1 7.8 %collective-permute-start.1 = (f32[64,4,128]{2,1,0:T(4,128)S(1)}, f32[64,4,128]{2,1,0:T(4,128)S(1)}, u32[]{:S(2)}, u32[]{:S(2)}) collective-permute-start(f32[64,4,128]{2,1,0:T(4,128)S(1)} %get-tuple-element.656), channel_id=1, source_target_pairs={{0,4},{4,8},{8,12},{12,16},{16,20},{20,24},{24,28},{28,0},{1,5},{5... | collective-permute-start | bytes 393224 | tf_op jit(solution)/shard_map/while/body/eval_jaxpr/ppermute | solution.py:20
  115.2 7.8 %collective-permute-start.1 = (f32[64,4,128]{2,1,0:T(4,128)S(1)}, f32[64,4,128]{2,1,0:T(4,128)S(1)}, u32[]{:S(2)}, u32[]{:S(2)}) collective-permute-start(f32[64,4,128]{2,1,0:T(4,128)S(1)} %get-tuple-element.656), channel_id=1, source_target_pairs={{0,4},{4,8},{8,12},{12,16},{16,20},{20,24},{24,28},{28,0},{1,5},{5... | collective-permute-start | bytes 393224 | tf_op jit(solution)/shard_map/while/body/eval_jaxpr/ppermute | solution.py:20
  123.4 8.0 %collective-permute-start.1 = (f32[64,4,128]{2,1,0:T(4,128)S(1)}, f32[64,4,128]{2,1,0:T(4,128)S(1)}, u32[]{:S(2)}, u32[]{:S(2)}) collective-permute-start(f32[64,4,128]{2,1,0:T(4,128)S(1)} %get-tuple-element.656), channel_id=1, source_target_pairs={{0,4},{4,8},{8,12},{12,16},{16,20},{20,24},{24,28},{28,0},{1,5},{5... | collective-permute-start | bytes 393224 | tf_op jit(solution)/shard_map/while/body/eval_jaxpr/ppermute | solution.py:20
  131.7 9.2 %collective-permute-start.1 = (f32[64,4,128]{2,1,0:T(4,128)S(1)}, f32[64,4,128]{2,1,0:T(4,128)S(1)}, u32[]{:S(2)}, u32[]{:S(2)}) collective-permute-start(f32[64,4,128]{2,1,0:T(4,128)S(1)} %get-tuple-element.656), channel_id=1, source_target_pairs={{0,4},{4,8},{8,12},{12,16},{16,20},{20,24},{24,28},{28,0},{1,5},{5... | collective-permute-start | bytes 393224 | tf_op jit(solution)/shard_map/while/body/eval_jaxpr/ppermute | solution.py:20
  141.3 7.7 %collective-permute-start.1 = (f32[64,4,128]{2,1,0:T(4,128)S(1)}, f32[64,4,128]{2,1,0:T(4,128)S(1)}, u32[]{:S(2)}, u32[]{:S(2)}) collective-permute-start(f32[64,4,128]{2,1,0:T(4,128)S(1)} %get-tuple-element.656), channel_id=1, source_target_pairs={{0,4},{4,8},{8,12},{12,16},{16,20},{20,24},{24,28},{28,0},{1,5},{5... | collective-permute-start | bytes 393224 | tf_op jit(solution)/shard_map/while/body/eval_jaxpr/ppermute | solution.py:20
Sparse Core Ops, SparseCore 0:
  88.1 122.0 all-reduce.1
